TPU v7x, 32 devices: a whole 2x2x4 slice. The times are simulated.
32 devices in a mesh: dp: 16 (over z, y, core), tensor: 2 (over x).
Axes of the slice: x: 2, y: 2, z: 4, core: 2. Of those that a mesh axis runs over, the one named last changes fastest.
Arguments:
- block_in: bfloat16 [16, 1024, 1024], P('dp', 'tensor'), may hold values from -50 to 50
- valid_count: int32 [16], P('dp'), may hold values from 512 to 1024, as said below
- vectors: float32 [14, 1024], P(None, ('dp', 'tensor')), may hold values from -2 to 2
- qkv_weight: bfloat16 [3, 1024, 1024], P(None, 'dp', 'tensor'), may hold values from -1.5 to 1.5
- out_weight: bfloat16 [1024, 1024], P('tensor', 'dp'), may hold values from -1.5 to 1.5
- up_weight: bfloat16 [1024, 4096], P('dp', 'tensor'), may hold values from -0.1875 to 0.1875
- down_weight: bfloat16 [4096, 1024], P('tensor', 'dp'), may hold values from -0.09375 to 0.09375
- cotangent: bfloat16 [16, 1024, 1024], P('dp', 'tensor'), may hold values from -6 to 6
Outputs:
- block_out: bfloat16 [16, 1024, 1024], P('dp', 'tensor')
- grad_input: float32 [16, 1024, 1024], P('dp', 'tensor')
- grad_vectors: float32 [14, 1024], P(None, ('dp', 'tensor'))
- grad_qkv: float32 [3, 1024, 1024], P(None, 'dp', 'tensor')
- grad_proj: float32 [1024, 1024], P('tensor', 'dp')
- grad_up: float32 [1024, 4096], P('dp', 'tensor')
- grad_down: float32 [4096, 1024], P('tensor', 'dp')
Inputs may be any that keep to these rules, and one draw needn't show every extreme that they name: Keys from position valid_count on are masked in their image; some image has all 1024 tokens valid.
All inputs are finite; a program needn't handle non-finite values.
Results may differ from a plain program's by a relative error of at most 0.019.
Values may be sent and summed in bfloat16 or wider, within the bound.
A program may use at most 192 MiB of HBM per device.

v0:
```python
import jax
import jax.numpy as jnp
from jax import lax
from jax.sharding import PartitionSpec as P

FF = 4096
HEAD = 64
NORM_EPS = 1e-06
ROOT_HALF = 0.7071067811865476
INV_ROOT_TAU = 0.3989422804014327
MASKED = -1e30


def layer_norm(values):
    center = values - jnp.mean(values, axis=-1, keepdims=True)
    inverse = lax.rsqrt(jnp.mean(center * center, axis=-1, keepdims=True) + NORM_EPS)
    return (center * inverse, inverse)


def norm_back(grad_hat, normed, inverse):
    first_mean = jnp.mean(grad_hat, axis=-1, keepdims=True)
    second_mean = jnp.mean(grad_hat * normed, axis=-1, keepdims=True)
    return inverse * (grad_hat - first_mean - normed * second_mean)


def gelu_pair(hidden):
    cumul = 0.5 * (1.0 + jax.scipy.special.erf(hidden * ROOT_HALF))
    density = jnp.exp(-0.5 * hidden * hidden) * INV_ROOT_TAU
    return (hidden * cumul, cumul + hidden * density)


def matmul(left_side, right_side):
    return jnp.dot(left_side, right_side, preferred_element_type=jnp.float32)


def times_transposed(left_side, right_side):
    return lax.dot_general(
        left_side, right_side, (((1,), (1,)), ((), ())), preferred_element_type=jnp.float32
    )


def transposed_times(left_side, right_side):
    return lax.dot_general(
        left_side, right_side, (((0,), (0,)), ((), ())), preferred_element_type=jnp.float32
    )


def masked_scores(queries, key_rows, visible, score_scale):
    scores = (
        jnp.einsum("qhe,khe->hqk", queries, key_rows, preferred_element_type=jnp.float32)
        * score_scale
    )
    return jnp.where(visible[None, None, :], scores, MASKED)


def attend(queries, key_rows, value_rows, visible, score_scale):
    scores = masked_scores(queries, key_rows, visible, score_scale)
    row_max = jnp.max(scores, axis=-1, keepdims=True)
    log_total = row_max + jnp.log(jnp.sum(jnp.exp(scores - row_max), axis=-1, keepdims=True))
    weights_low = jnp.exp(scores - log_total).astype(jnp.bfloat16)
    mixed = jnp.einsum("hqk,khe->qhe", weights_low, value_rows, preferred_element_type=jnp.float32)
    return (mixed.astype(jnp.bfloat16), log_total)


def attend_back(queries, key_rows, value_rows, mixed, grad_mixed, log_total, visible, score_scale):
    probs = jnp.exp(masked_scores(queries, key_rows, visible, score_scale) - log_total)
    probs_low = probs.astype(jnp.bfloat16)
    grad_values = jnp.einsum(
        "hqk,qhe->khe", probs_low, grad_mixed, preferred_element_type=jnp.float32
    )
    grad_probs = jnp.einsum(
        "qhe,khe->hqk", grad_mixed, value_rows, preferred_element_type=jnp.float32
    )
    delta = jnp.einsum("qhe,qhe->hq", grad_mixed, mixed, preferred_element_type=jnp.float32)[
        :, :, None
    ]
    grad_scores = (probs * (grad_probs - delta)).astype(jnp.bfloat16)
    grad_queries = score_scale * jnp.einsum(
        "hqk,khe->qhe", grad_scores, key_rows, preferred_element_type=jnp.float32
    )
    grad_keys = score_scale * jnp.einsum(
        "hqk,qhe->khe", grad_scores, queries, preferred_element_type=jnp.float32
    )
    return (grad_queries, grad_keys, grad_values)


def gather_rows(shard_low):
    return lax.all_gather(shard_low, "tensor", axis=0, tiled=True)


def gather_cotangent(shard_low):
    return lax.all_gather(shard_low, "tensor", axis=0, tiled=True)


def pair_sum(factor_pairs, product):
    running = None
    for left_side, right_side in factor_pairs:
        addend = product(left_side, right_side)
        running = addend if running is None else running + addend
    return running


def branch_rows(factor_pairs):
    return lax.psum_scatter(
        pair_sum(factor_pairs, matmul).astype(jnp.bfloat16),
        "tensor",
        scatter_dimension=0,
        tiled=True,
    ).astype(jnp.float32)


def back_rows(factor_pairs):
    return lax.psum_scatter(
        pair_sum(factor_pairs, times_transposed).astype(jnp.bfloat16),
        "tensor",
        scatter_dimension=0,
        tiled=True,
    ).astype(jnp.float32)


def local(
    block_in, valid_count, vectors, qkv_weight, out_weight, up_weight, down_weight, cotangent
):
    params = lax.all_gather(vectors, ("dp", "tensor"), axis=1, tiled=True)
    qkv_full, out_full, up_full, down_full = (
        lax.all_gather(qkv_weight, "dp", axis=1, tiled=True),
        lax.all_gather(out_weight, "dp", axis=1, tiled=True),
        lax.all_gather(up_weight, "dp", axis=0, tiled=True),
        lax.all_gather(down_weight, "dp", axis=1, tiled=True),
    )
    model_width = params.shape[1]
    local_width = qkv_full.shape[2]
    local_units = up_full.shape[1]
    local_heads = local_width // HEAD
    shard_rows = block_in.shape[1]
    seq_len = shard_rows * lax.axis_size("tensor")
    tensor_rank = lax.axis_index("tensor")
    score_scale = HEAD ** (-0.5)
    (
        gain_one,
        shift_one,
        query_bias_all,
        value_bias_all,
        bias_out,
        scale_one,
        gain_two,
        shift_two,
        bias_down,
        scale_two,
    ) = params[:10]
    bias_query = lax.dynamic_slice_in_dim(query_bias_all, tensor_rank * local_width, local_width)
    bias_value = lax.dynamic_slice_in_dim(value_bias_all, tensor_rank * local_width, local_width)
    bias_up = lax.dynamic_slice_in_dim(
        params[10:].reshape(-1), tensor_rank * local_units, local_units
    )
    positions = lax.iota(jnp.int32, seq_len)
    zero_row = jnp.zeros((model_width,), jnp.float32)
    input_rows = block_in[0].astype(jnp.float32)
    normed_one, inverse_one = layer_norm(input_rows)
    hidden_one = gather_rows((normed_one * gain_one + shift_one).astype(jnp.bfloat16))
    queries = (
        (matmul(hidden_one, qkv_full[0]) + bias_query)
        .astype(jnp.bfloat16)
        .reshape(seq_len, local_heads, HEAD)
    )
    key_rows = (
        matmul(hidden_one, qkv_full[1]).astype(jnp.bfloat16).reshape(seq_len, local_heads, HEAD)
    )
    value_rows = (
        (matmul(hidden_one, qkv_full[2]) + bias_value)
        .astype(jnp.bfloat16)
        .reshape(seq_len, local_heads, HEAD)
    )
    visible = positions < valid_count[0]
    mixed, log_total = attend(queries, key_rows, value_rows, visible, score_scale)
    mixed_flat = mixed.reshape(seq_len, local_width)
    branch_one = branch_rows(((mixed_flat, out_full),)) + bias_out
    middle = input_rows + scale_one * branch_one
    normed_two, inverse_two = layer_norm(middle)
    hidden_two = gather_rows((normed_two * gain_two + shift_two).astype(jnp.bfloat16))
    activated, gelu_slope = gelu_pair(matmul(hidden_two, up_full) + bias_up)
    act_low = activated.astype(jnp.bfloat16)
    branch_two = branch_rows(((act_low, down_full),)) + bias_down
    out_list = [(middle + scale_two * branch_two).astype(jnp.bfloat16)]
    grad_rows = cotangent[0].astype(jnp.float32)
    grad_scale_two = jnp.sum(grad_rows * branch_two, axis=0)
    grad_bias_down = jnp.sum(grad_rows * scale_two, axis=0)
    grad_branch_two = gather_cotangent((grad_rows * scale_two).astype(jnp.bfloat16))
    grad_down = transposed_times(act_low, grad_branch_two)
    grad_pre = times_transposed(grad_branch_two, down_full) * gelu_slope
    grad_bias_up = jnp.sum(grad_pre, axis=0)
    grad_pre_low = grad_pre.astype(jnp.bfloat16)
    grad_up = transposed_times(hidden_two, grad_pre_low)
    grad_hidden_two = back_rows(((grad_pre_low, up_full),))
    grad_gain_two = jnp.sum(grad_hidden_two * normed_two, axis=0)
    grad_shift_two = jnp.sum(grad_hidden_two, axis=0)
    grad_middle = grad_rows + norm_back(grad_hidden_two * gain_two, normed_two, inverse_two)
    grad_scale_one = jnp.sum(grad_middle * branch_one, axis=0)
    grad_bias_out = jnp.sum(grad_middle * scale_one, axis=0)
    grad_branch_one = gather_cotangent((grad_middle * scale_one).astype(jnp.bfloat16))
    grad_proj_sum = transposed_times(mixed_flat, grad_branch_one)
    grad_mixed = (
        times_transposed(grad_branch_one, out_full)
        .astype(jnp.bfloat16)
        .reshape(seq_len, local_heads, HEAD)
    )
    grad_queries, grad_keys, grad_values = attend_back(
        queries, key_rows, value_rows, mixed, grad_mixed, log_total, visible, score_scale
    )
    grad_queries = grad_queries.reshape(seq_len, local_width)
    grad_keys = grad_keys.reshape(seq_len, local_width)
    grad_values = grad_values.reshape(seq_len, local_width)
    grad_bias_query = jnp.sum(grad_queries, axis=0)
    grad_bias_value = jnp.sum(grad_values, axis=0)
    query_low = grad_queries.astype(jnp.bfloat16)
    key_low = grad_keys.astype(jnp.bfloat16)
    value_low = grad_values.astype(jnp.bfloat16)
    grad_qkv_sum = jnp.stack(
        [
            transposed_times(hidden_one, query_low),
            transposed_times(hidden_one, key_low),
            transposed_times(hidden_one, value_low),
        ]
    )
    grad_hidden_one = back_rows(
        ((query_low, qkv_full[0]), (key_low, qkv_full[1]), (value_low, qkv_full[2]))
    )
    grad_gain_one = jnp.sum(grad_hidden_one * normed_one, axis=0)
    grad_shift_one = jnp.sum(grad_hidden_one, axis=0)
    grad_list = [grad_middle + norm_back(grad_hidden_one * gain_one, normed_one, inverse_one)]
    placed_query = lax.dynamic_update_slice_in_dim(
        zero_row, grad_bias_query, tensor_rank * local_width, 0
    )
    placed_value = lax.dynamic_update_slice_in_dim(
        zero_row, grad_bias_value, tensor_rank * local_width, 0
    )
    placed_up = lax.dynamic_update_slice_in_dim(
        jnp.zeros((FF,), jnp.float32), grad_bias_up, tensor_rank * local_units, 0
    )
    image_params = jnp.concatenate(
        [
            jnp.stack(
                [
                    grad_gain_one,
                    grad_shift_one,
                    placed_query,
                    placed_value,
                    grad_bias_out,
                    grad_scale_one,
                    grad_gain_two,
                    grad_shift_two,
                    grad_bias_down,
                    grad_scale_two,
                ]
            ),
            placed_up.reshape(-1, model_width),
        ],
        axis=0,
    )
    owned_qkv, owned_proj, owned_up, owned_down = (
        lax.psum_scatter(
            grad_qkv_sum.astype(jnp.bfloat16), "dp", scatter_dimension=1, tiled=True
        ).astype(jnp.float32),
        lax.psum_scatter(
            grad_proj_sum.astype(jnp.bfloat16), "dp", scatter_dimension=1, tiled=True
        ).astype(jnp.float32),
        lax.psum_scatter(
            grad_up.astype(jnp.bfloat16), "dp", scatter_dimension=0, tiled=True
        ).astype(jnp.float32),
        lax.psum_scatter(
            grad_down.astype(jnp.bfloat16), "dp", scatter_dimension=1, tiled=True
        ).astype(jnp.float32),
    )
    owned_params = lax.psum_scatter(image_params, ("dp", "tensor"), scatter_dimension=1, tiled=True)
    return (
        jnp.stack(out_list),
        jnp.stack(grad_list),
        owned_params,
        owned_qkv,
        owned_proj,
        owned_up,
        owned_down,
    )


def solution(mesh):
    placed = (
        P("dp", "tensor", None),
        P("dp"),
        P(None, ("dp", "tensor")),
        P(None, "dp", "tensor"),
        P("tensor", "dp"),
        P("dp", "tensor"),
        P("tensor", "dp"),
        P("dp", "tensor", None),
    )
    return jax.shard_map(
        local,
        mesh=mesh,
        in_specs=placed,
        out_specs=(
            P("dp", "tensor", None),
            P("dp", "tensor", None),
            P(None, ("dp", "tensor")),
            P(None, "dp", "tensor"),
            P("tensor", "dp"),
            P("dp", "tensor"),
            P("tensor", "dp"),
        ),
        check_vma=False,
    )
```

profile of v0, /device:TPU:0, one launch (start us, length us, event | category | flops | bytes accessed | tf_op | source)
XLA Modules:
  0.0 1073.9 jit_solution(8662764909699897277)
XLA Ops:
  7.2 71.4 %all-gather = f32[32,32,14]{1,2,0:T(8,128)S(1)} all-gather(f32[1,32,14]{1,2,0:T(8,128)} %bitcast.230), channel_id=1, replica_groups=mesh['dp'=16,'tensor'=2] {'dp','tensor'}, dimensions={0}, use_global_device_ids=true | all-gather | bytes 59136 | tf_op jit(solution)/shard_map/all_gather | solution.py:124
  84.5 26.9 %all-gather.10.cloned.1.call-done = bf16[1024,1024]{1,0:T(8,128)(2,1)} async-done(((bf16[512,1024]{1,0:T(8,128)(2,1)}), bf16[1024,1024]{1,0:T(8,128)(2,1)}) %all-gather.10.cloned.1.call-update) | async-done | bytes 2097168 | tf_op jit(solution)/shard_map/all_gather | solution.py:88
  111.4 47.7 %all-gather.12.cloned.1.call-done = bf16[3,1024,512]{2,1,0:T(8,128)(2,1)} async-done(((bf16[3,64,512]{2,1,0:T(8,128)(2,1)}), bf16[3,1024,512]{2,1,0:T(8,128)(2,1)}) %all-gather.12.cloned.1.call-update) | async-done | bytes 3145744 | tf_op jit(solution)/shard_map/all_gather | solution.py:126
  164.0 14.1 %fusion.1 = (f32[8,1024]{1,0:T(8,128)S(1)}, f32[8,1024,1024]{1,2,0:T(8,128)}) fusion(pred[1024]{0:T(1024)(128)(4,1)S(1)} %iota_compare_fusion, bf16[1024,8,64]{0,2,1:T(8,128)(2,1)S(1)} %bitcast.181, bf16[1024,8,64]{0,2,1:T(8,128)(2,1)S(1)} %bitcast.179), kind=kOutput, calls=%fused_computation.5 | convolution fusion | flops 1098899456 | bytes 35685376 | tf_op jit(solution)/shard_map/qhe,khe->hqk/dot_general | solution.py:50
  178.1 15.1 %exponential_reduce_fusion = f32[8,1024]{1,0:T(8,128)S(1)} fusion(f32[8,1024,1024]{1,2,0:T(8,128)} %get-tuple-element.34, f32[8,1024]{1,0:T(8,128)S(1)} %get-tuple-element.33, pred[1024]{0:T(1024)(128)(4,1)S(1)} %iota_compare_fusion), kind=kLoop, calls=%fused_computation.2 | loop fusion | flops 33546240 | bytes 33620992 | tf_op jit(solution)/shard_map/reduce_sum | solution.py:59
  225.7 29.8 %reduce-scatter.12.cloned.1.call-done = bf16[512,1024]{1,0:T(8,128)(2,1)} async-done(((bf16[1024,1024]{1,0:T(8,128)(2,1)}), bf16[512,1024]{1,0:T(8,128)(2,1)}) %reduce-scatter.12.cloned.1.call-update) | async-done | bytes 1048592 | tf_op jit(solution)/shard_map/reduce_scatter | solution.py:104
  262.2 45.6 %all-gather.18.cloned.1.call-done = bf16[1024,2048]{1,0:T(8,128)(2,1)} async-done(((bf16[64,2048]{1,0:T(8,128)(2,1)}), bf16[1024,2048]{1,0:T(8,128)(2,1)}) %all-gather.18.cloned.1.call-update) | async-done | bytes 4194320 | tf_op jit(solution)/shard_map/all_gather | solution.py:128
  307.9 33.6 %all-gather.16.cloned.1.call-done = bf16[1024,1024]{1,0:T(8,128)(2,1)} async-done(((bf16[512,1024]{1,0:T(8,128)(2,1)}), bf16[1024,1024]{1,0:T(8,128)(2,1)}) %all-gather.16.cloned.1.call-update) | async-done | bytes 2097168 | tf_op jit(solution)/shard_map/all_gather | solution.py:88
  341.5 10.1 multiply_convert_fusion.1
  351.6 25.1 %all-gather.22.cloned.1.call-done = bf16[1024,1024]{1,0:T(8,128)(2,1)} async-done(((bf16[512,1024]{1,0:T(8,128)(2,1)}), bf16[1024,1024]{1,0:T(8,128)(2,1)}) %all-gather.22.cloned.1.call-update) | async-done | bytes 2097168 | tf_op jit(solution)/shard_map/all_gather | solution.py:92
  376.7 52.6 %all-gather.20.cloned.1.call-done = bf16[2048,1024]{0,1:T(8,128)(2,1)} async-done(((bf16[2048,64]{0,1:T(8,128)(2,1)}), bf16[2048,1024]{0,1:T(8,128)(2,1)}) %all-gather.20.cloned.1.call-update) | async-done | bytes 4194320 | tf_op jit(solution)/shard_map/all_gather | solution.py:129
  429.3 10.8 %fusion.50 = (f32[2048]{0:T(1024)S(1)}, bf16[1024,2048]{1,0:T(8,128)(2,1)S(1)}) fusion(f32[1024,2048]{1,0:T(8,128)} %get-tuple-element.36, f32[2048]{0:T(1024)S(1)} %dynamic_slice.11, bf16[1024,1024]{1,0:T(8,128)(2,1)} %all-gather.22.cloned.1.call-done, bf16[2048,1024]{0,1:T(8,128)(2,1)} %all-gather.20.cloned.1.call-done), kind=kOutput, calls=%fused_computation.115 | convolution fusion | flops 4320131072 | bytes 18890752 | tf_op jit(solution)/shard_map/dot_general | solution.py:37
  457.4 21.0 %reduce-scatter.16.cloned.1.call-done = bf16[512,1024]{1,0:T(8,128)(2,1)} async-done(((bf16[1024,1024]{1,0:T(8,128)(2,1)}), bf16[512,1024]{1,0:T(8,128)(2,1)}) %reduce-scatter.16.cloned.1.call-update) | async-done | bytes 1048592 | tf_op jit(solution)/shard_map/reduce_scatter | solution.py:113
  480.9 31.5 %reduce-scatter.14.cloned.1.call-done = bf16[512,1024]{1,0:T(8,128)(2,1)} async-done(((bf16[1024,1024]{1,0:T(8,128)(2,1)}), bf16[512,1024]{1,0:T(8,128)(2,1)}) %reduce-scatter.14.cloned.1.call-update) | async-done | bytes 1048592 | tf_op jit(solution)/shard_map/reduce_scatter | solution.py:104
  519.5 33.2 %all-gather.24.cloned.1.call-done = bf16[1024,1024]{1,0:T(8,128)(2,1)} async-done(((bf16[512,1024]{1,0:T(8,128)(2,1)}), bf16[1024,1024]{1,0:T(8,128)(2,1)}) %all-gather.24.cloned.1.call-update) | async-done | bytes 2097168 | tf_op jit(solution)/shard_map/all_gather | solution.py:92
  556.6 12.3 %bitcast_convert_fusion = (bf16[1024,8,64]{0,2,1:T(8,128)(2,1)}, f32[8,64,1024]{2,1,0:T(8,128)S(1)}) fusion(bf16[1024,8,64]{0,2,1:T(8,128)(2,1)} %bitcast.194, bf16[8,1024,1024]{1,2,0:T(8,128)(2,1)} %fusion), kind=kOutput, calls=%fused_computation.58 | convolution fusion | flops 1074266112 | bytes 20971520 | tf_op jit(solution)/shard_map/hqk,qhe->khe/dot_general | solution.py:68
  568.9 21.1 %multiply_convert_fusion = bf16[8,1024,1024]{1,2,0:T(8,128)(2,1)} fusion(f32[8,1024,1024]{1,2,0:T(8,128)} %get-tuple-element.34, f32[8,1024]{1,0:T(8,128)S(1)} %get-tuple-element.37, f32[8,1024]{1,0:T(8,128)S(1)} %log_add_fusion, pred[1024]{0:T(1024)(128)(4,1)S(1)} %iota_compare_fusion, bf16[1024,8,64]{0,2,1:T(8,128)(2,1)} %bitcast.195, ...), kind=kOutput, calls=%fused_computation | convolution fusion | flops 1124073472 | bytes 52495360 | tf_op jit(solution)/shard_map/qhe,khe->hqk/dot_general | solution.py:71
  590.0 12.3 %multiply_convert_fusion.2 = bf16[8,64,1024]{2,1,0:T(8,128)(2,1)} fusion(bf16[1024,8,64]{0,2,1:T(8,128)(2,1)} %bitcast.182, bf16[8,1024,1024]{1,2,0:T(8,128)(2,1)} %multiply_convert_fusion), kind=kOutput, calls=%fused_computation.64 | convolution fusion | flops 1074790400 | bytes 18874368 | tf_op jit(solution)/shard_map/hqk,qhe->khe/dot_general | solution.py:81
  602.3 10.6 bitcast_convert_fusion.1
  658.0 68.9 %reduce-scatter.24.cloned.1.call-done = bf16[64,2048]{1,0:T(8,128)(2,1)} async-done(((bf16[1024,2048]{1,0:T(8,128)(2,1)}), bf16[64,2048]{1,0:T(8,128)(2,1)}) %reduce-scatter.24.cloned.1.call-update) | async-done | bytes 262160 | tf_op jit(solution)/shard_map/reduce_scatter | solution.py:267
  728.7 73.8 %reduce-scatter.26.cloned.1.call-done = bf16[2048,64]{0,1:T(8,128)(2,1)} async-done(((bf16[2048,1024]{0,1:T(8,128)(2,1)}), bf16[2048,64]{0,1:T(8,128)(2,1)}) %reduce-scatter.26.cloned.1.call-update) | async-done | bytes 262160 | tf_op jit(solution)/shard_map/reduce_scatter | solution.py:270
  804.2 58.3 %reduce-scatter.22.cloned.1.call-done = bf16[512,64]{0,1:T(8,128)(2,1)} async-done(((bf16[512,1024]{0,1:T(8,128)(2,1)}), bf16[512,64]{0,1:T(8,128)(2,1)}) %reduce-scatter.22.cloned.1.call-update) | async-done | bytes 65552 | tf_op jit(solution)/shard_map/reduce_scatter | solution.py:264
  867.4 132.2 %reduce-scatter.28.cloned.1.call-done = f32[32,14]{1,0:T(8,128)} async-done(((f32[1024,14]{1,0:T(8,128)}), f32[32,14]{1,0:T(8,128)}) %reduce-scatter.28.cloned.1.call-update) | async-done | bytes 1808
  1000.9 64.6 %reduce-scatter.20.cloned.1.call-done = bf16[3,64,512]{2,1,0:T(8,128)(2,1)} async-done(((bf16[3,1024,512]{2,1,0:T(8,128)(2,1)}), bf16[3,64,512]{2,1,0:T(8,128)(2,1)}) %reduce-scatter.20.cloned.1.call-update) | async-done | bytes 196624 | tf_op jit(solution)/shard_map/reduce_scatter | solution.py:261
  (164 shorter events, 136.1 us)
Async XLA Ops:
  7.2 73.2 %copy-start.1 = (bf16[1,512,1024]{2,1,0:T(8,128)(2,1)S(1)}, bf16[1,512,1024]{2,1,0:T(8,128)(2,1)}, u32[]{:S(2)}) copy-start(bf16[1,512,1024]{2,1,0:T(8,128)(2,1)} %param.8) | copy-start | bytes 3145732
  7.2 104.2 %all-gather.10.cloned.1.call-start = ((), (), s32[]{:S(2)}) async-start(), calls=%async_computation.9 | async-start | bytes 3145728 | tf_op jit(solution)/shard_map/all_gather | solution.py:88
  80.8 81.6 %copy-start.24 = (f32[512]{0:T(512)}, f32[512]{0:T(512)S(1)}, u32[]{:S(2)}) copy-start(f32[512]{0:T(512)S(1)} %add_rsqrt_fusion.1) | copy-start | bytes 6148
  82.3 76.8 %all-gather.12.cloned.1.call-start = ((), (), s32[]{:S(2)}) async-start(), calls=%async_computation.10 | async-start | bytes 3342336 | tf_op jit(solution)/shard_map/all_gather | solution.py:126
  83.0 137.7 %all-gather.14.cloned.1.call-start = ((), (), s32[]{:S(2)}) async-start(), calls=%async_computation.11 | async-start | bytes 1114112 | tf_op jit(solution)/shard_map/all_gather | solution.py:127
  83.8 171.7 %reduce-scatter.12.cloned.1.call-start = ((), (), s32[]{:S(2)}) async-start(), calls=%async_computation.12 | async-start | bytes 3145728 | tf_op jit(solution)/shard_map/reduce_scatter | solution.py:104
  163.9 14.1 %copy-start.6 = (bf16[1024,512]{0,1:T(8,128)(2,1)}, bf16[1024,512]{0,1:T(8,128)(2,1)S(1)}, u32[]{:S(2)}) copy-start(bf16[1024,512]{0,1:T(8,128)(2,1)S(1)} %add_convert_fusion.3) | copy-start | bytes 3145732
  178.1 20.5 %copy-start = (f32[8,1024,1024]{1,2,0:T(8,128)S(1)}, f32[8,1024,1024]{1,2,0:T(8,128)}, u32[]{:S(2)}) copy-start(f32[8,1024,1024]{1,2,0:T(8,128)} %get-tuple-element.34) | copy-start | bytes 100663296
  225.0 82.8 %all-gather.18.cloned.1.call-start = ((), (), s32[]{:S(2)}) async-start(), calls=%async_computation.14 | async-start | bytes 4456448 | tf_op jit(solution)/shard_map/all_gather | solution.py:128
  225.6 115.9 %all-gather.16.cloned.1.call-start = ((), (), s32[]{:S(2)}) async-start(), calls=%async_computation.13 | async-start | bytes 3145728 | tf_op jit(solution)/shard_map/all_gather | solution.py:88
  259.6 117.2 %all-gather.22.cloned.1.call-start = ((), (), s32[]{:S(2)}) async-start(), calls=%async_computation.17 | async-start | bytes 3145728 | tf_op jit(solution)/shard_map/all_gather | solution.py:92
  261.4 167.9 %all-gather.20.cloned.1.call-start = ((), (), s32[]{:S(2)}) async-start(), calls=%async_computation.15 | async-start | bytes 4456448 | tf_op jit(solution)/shard_map/all_gather | solution.py:129
  262.1 216.3 %reduce-scatter.16.cloned.1.call-start = ((), (), s32[]{:S(2)}) async-start(), calls=%async_computation.18 | async-start | bytes 3145728 | tf_op jit(solution)/shard_map/reduce_scatter | solution.py:113
  447.9 64.6 %reduce-scatter.14.cloned.1.call-start = ((), (), s32[]{:S(2)}) async-start(), calls=%async_computation.16 | async-start | bytes 3145728 | tf_op jit(solution)/shard_map/reduce_scatter | solution.py:104
  457.2 95.5 %all-gather.24.cloned.1.call-start = ((), (), s32[]{:S(2)}) async-start(), calls=%async_computation.19 | async-start | bytes 3145728 | tf_op jit(solution)/shard_map/all_gather | solution.py:92
  518.2 34.5 %copy-start.11 = (bf16[8,64,1024]{2,1,0:T(8,128)(2,1)S(1)}, bf16[8,64,1024]{2,1,0:T(8,128)(2,1)}, u32[]{:S(2)}) copy-start(bf16[8,64,1024]{2,1,0:T(8,128)(2,1)} %copy-done.10) | copy-start | bytes 3145732
  518.2 34.5 %copy-start.29 = (bf16[512,1024]{0,1:T(8,128)(2,1)S(1)}, bf16[512,1024]{0,1:T(8,128)(2,1)}, u32[]{:S(2)}) copy-start(bf16[512,1024]{0,1:T(8,128)(2,1)} %all-gather.14.cloned.1.call-done) | copy-start | bytes 3145732
  519.5 131.8 %reduce-scatter.18.cloned.1.call-start = ((), (), s32[]{:S(2)}) async-start(), calls=%async_computation.20 | async-start | bytes 3145728 | tf_op jit(solution)/shard_map/reduce_scatter | solution.py:113
  618.2 108.7 %reduce-scatter.24.cloned.1.call-start = ((), (), s32[]{:S(2)}) async-start(), calls=%async_computation.23 | async-start | bytes 4456448 | tf_op jit(solution)/shard_map/reduce_scatter | solution.py:267
  628.1 174.4 %reduce-scatter.26.cloned.1.call-start = ((), (), s32[]{:S(2)}) async-start(), calls=%async_computation.24 | async-start | bytes 4456448 | tf_op jit(solution)/shard_map/reduce_scatter | solution.py:270
  637.5 225.0 %reduce-scatter.22.cloned.1.call-start = ((), (), s32[]{:S(2)}) async-start(), calls=%async_computation.22 | async-start | bytes 1114112 | tf_op jit(solution)/shard_map/reduce_scatter | solution.py:264
  644.1 355.4 %reduce-scatter.28.cloned.1.call-start = ((), (), s32[]{:S(2)}) async-start(), calls=%async_computation.25 | async-start | bytes 540672
  654.7 410.8 %reduce-scatter.20.cloned.1.call-start = ((), (), s32[]{:S(2)}) async-start(), calls=%async_computation.21 | async-start | bytes 3342336 | tf_op jit(solution)/shard_map/reduce_scatter | solution.py:261
  657.9 206.1 %copy-start.4 = (f32[512,1024]{1,0:T(8,128)S(1)}, f32[512,1024]{1,0:T(8,128)}, u32[]{:S(2)}) copy-start(f32[512,1024]{1,0:T(8,128)} %copy-done.3) | copy-start | bytes 6291460
  (24 other events, 83.7 us)
Sparse Core Ops, SparseCore 0:
  82.4 28.9 all-gather.9
  113.6 45.4 all-gather.11
  161.3 36.2 all-gather.13
  225.1 30.2 reduce-scatter.11
  257.4 50.3 all-gather.17
  309.8 31.6 all-gather.15
  343.6 33.0 all-gather.21
  378.9 50.3 all-gather.19
  448.0 30.4 reduce-scatter.15
  480.5 31.8 reduce-scatter.13
  519.6 33.0 all-gather.23
  618.3 31.8 reduce-scatter.17
  654.1 72.7 reduce-scatter.23
  730.6 71.7 reduce-scatter.25
  805.9 56.5 reduce-scatter.21
  864.7 134.8 reduce-scatter.27
  1003.2 62.2 reduce-scatter.19
where the time goes:
time: 1080 us; the launch traced here: 1070 us
  waiting for transfers between devices  748 us (69%)
  matrix products  165 us (15%)
  blocking collectives  71.4 us (7%)
  other arithmetic  59 us (5%)
  between operations  15.3 us (1%)
  local copies, waits for them, and re-layouts  13.2 us (1%)
    unnamed x18, waiting for transfers between devices  135 us
    reduce_scatter x1, waiting for transfers between devices, local(): lax.psum_scatter(grad_down.astype(jnp.bfloat16), 'dp', scatter_dimension=...  73.8 us
    all_gather x1, blocking collectives, local(): params = lax.all_gather(vectors, ('dp', 'tensor'), axis=1, tiled=True)  71.4 us
    reduce_scatter x1, waiting for transfers between devices, local(): lax.psum_scatter(grad_up.astype(jnp.bfloat16), 'dp', scatter_dimension=0,...  68.9 us
    reduce_scatter x1, waiting for transfers between devices, local(): lax.psum_scatter(grad_qkv_sum.astype(jnp.bfloat16), 'dp', scatter_dimensi...  64.6 us
    reduce_scatter x2, waiting for transfers between devices, branch_rows(): lax.psum_scatter(pair_sum(factor_pairs, matmul).astype(jnp.bfloat16), 'te...  61.3 us
    all_gather x2, waiting for transfers between devices, gather_rows(): return lax.all_gather(shard_low, 'tensor', axis=0, tiled=True)  60.5 us
    reduce_scatter x1, waiting for transfers between devices, local(): lax.psum_scatter(grad_proj_sum.astype(jnp.bfloat16), 'dp', scatter_dimens...  58.3 us
  transfers between devices with their start and end apart: 17, of which 15 were waited for; matrix products, arithmetic and copies ran while one was open for 12% of the time, Pallas kernels for 0%

commit v1 on v0

--- a/solution.py
+++ b/solution.py
@@ -9,6 +9,18 @@
 ROOT_HALF = 0.7071067811865476
 INV_ROOT_TAU = 0.3989422804014327
 MASKED = -1e30
+
+
+def gather_by_bits(x, axis, dim):
+    ways, here, hop = (lax.axis_size(axis), lax.axis_index(axis), x.shape[dim])
+    line, have = (x, 1)
+    while have < ways:
+        line = jnp.concatenate(
+            [line, lax.ppermute(line, axis, [(d, (d - have) % ways) for d in range(ways)])],
+            axis=dim,
+        )
+        have = 2 * have
+    return jnp.roll(line, here * hop, axis=dim)
 
 
 def layer_norm(values):
@@ -89,7 +101,7 @@
 
 
 def gather_cotangent(shard_low):
-    return lax.all_gather(shard_low, "tensor", axis=0, tiled=True)
+    return gather_by_bits(shard_low, "tensor", 0)
 
 
 def pair_sum(factor_pairs, product):

time: 1080 us -> 1040 us (0.963)
  waiting for transfers between devices: 748 us -> 688 us
  starting transfers between devices: 1.97 us -> 12.9 us
    all_gather x2 -> x0, waiting for transfers between devices: 58.3 us -> none  [gather_cotangent(): return lax.all_gather(shard_low, 'tensor', axis=0, tiled=True)]
    ppermute x0 -> x2, waiting for transfers between devices: none -> 49 us  [gather_by_bits(): lax.ppermute(line, axis, [(d, (d - have) % ways) for d in range(ways)])]
    all_gather x1, waiting for transfers between devices: 45.6 us -> 4.42 us  [local(): lax.all_gather(up_weight, 'dp', axis=0, tiled=True)]
    reduce_scatter x2, starting transfers between devices: 0.08 us -> 11.1 us  [back_rows(): lax.psum_scatter(pair_sum(factor_pairs, times_transposed).astype(jnp.bflo...]
    unnamed x18 -> x16, waiting for transfers between devices: 135 us -> 135 us
  transfers between devices with their start and end apart: 17 -> 17, of which waited for: 15 -> 15; matrix products, arithmetic and copies ran while one was open for 12% -> 13% of each run, Pallas kernels for 0% -> 0%
where the time goes in v1:
time: 1040 us; the launch traced here: 1030 us
  waiting for transfers between devices  688 us (66%)
  matrix products  164 us (16%)
  blocking collectives  71.4 us (7%)
  other arithmetic  69 us (7%)
  between operations  15.4 us (1%)
  local copies, waits for them, and re-layouts  13.2 us (1%)
  starting transfers between devices  12.9 us (1%)
    unnamed x16, waiting for transfers between devices  135 us
    reduce_scatter x1, waiting for transfers between devices, local(): lax.psum_scatter(grad_down.astype(jnp.bfloat16), 'dp', scatter_dimension=...  73.8 us
    all_gather x1, blocking collectives, local(): params = lax.all_gather(vectors, ('dp', 'tensor'), axis=1, tiled=True)  71.4 us
    reduce_scatter x1, waiting for transfers between devices, local(): lax.psum_scatter(grad_up.astype(jnp.bfloat16), 'dp', scatter_dimension=0,...  69.2 us
    reduce_scatter x1, waiting for transfers between devices, local(): lax.psum_scatter(grad_qkv_sum.astype(jnp.bfloat16), 'dp', scatter_dimensi...  64.7 us
    reduce_scatter x2, waiting for transfers between devices, branch_rows(): lax.psum_scatter(pair_sum(factor_pairs, matmul).astype(jnp.bfloat16), 'te...  61.5 us
    all_gather x2, waiting for transfers between devices, gather_rows(): return lax.all_gather(shard_low, 'tensor', axis=0, tiled=True)  60.5 us
    reduce_scatter x1, waiting for transfers between devices, local(): lax.psum_scatter(grad_proj_sum.astype(jnp.bfloat16), 'dp', scatter_dimens...  58.4 us
  transfers between devices with their start and end apart: 17, of which 15 were waited for; matrix products, arithmetic and copies ran while one was open for 13% of the time, Pallas kernels for 0%

profile of v1, /device:TPU:0, one launch (start us, length us, event | category | flops | bytes accessed | tf_op | source)
XLA Modules:
  0.0 1033.3 jit_solution(15055348844627080580)
XLA Ops:
  7.2 71.4 %all-gather = f32[32,32,14]{1,2,0:T(8,128)S(1)} all-gather(f32[1,32,14]{1,2,0:T(8,128)} %bitcast.230), channel_id=1, replica_groups=mesh['dp'=16,'tensor'=2] {'dp','tensor'}, dimensions={0}, use_global_device_ids=true | all-gather | bytes 59136 | tf_op jit(solution)/shard_map/all_gather | solution.py:136
  84.5 26.9 %all-gather.8.cloned.1.call-done = bf16[1024,1024]{1,0:T(8,128)(2,1)} async-done(((bf16[512,1024]{1,0:T(8,128)(2,1)}), bf16[1024,1024]{1,0:T(8,128)(2,1)}) %all-gather.8.cloned.1.call-update) | async-done | bytes 2097168 | tf_op jit(solution)/shard_map/all_gather | solution.py:100
  111.4 47.7 %all-gather.10.cloned.1.call-done = bf16[3,1024,512]{2,1,0:T(8,128)(2,1)} async-done(((bf16[3,64,512]{2,1,0:T(8,128)(2,1)}), bf16[3,1024,512]{2,1,0:T(8,128)(2,1)}) %all-gather.10.cloned.1.call-update) | async-done | bytes 3145744 | tf_op jit(solution)/shard_map/all_gather | solution.py:138
  164.0 14.2 %fusion.1 = (f32[8,1024]{1,0:T(8,128)S(1)}, f32[8,1024,1024]{1,2,0:T(8,128)}) fusion(pred[1024]{0:T(1024)(128)(4,1)S(1)} %iota_compare_fusion, bf16[1024,8,64]{0,2,1:T(8,128)(2,1)S(1)} %bitcast.181, bf16[1024,8,64]{0,2,1:T(8,128)(2,1)S(1)} %bitcast.179), kind=kOutput, calls=%fused_computation.5 | convolution fusion | flops 1098899456 | bytes 35685376 | tf_op jit(solution)/shard_map/qhe,khe->hqk/dot_general | solution.py:62
  178.1 15.2 %exponential_reduce_fusion = f32[8,1024]{1,0:T(8,128)S(1)} fusion(f32[8,1024,1024]{1,2,0:T(8,128)} %get-tuple-element.35, f32[8,1024]{1,0:T(8,128)S(1)} %get-tuple-element.34, pred[1024]{0:T(1024)(128)(4,1)S(1)} %iota_compare_fusion), kind=kLoop, calls=%fused_computation.2 | loop fusion | flops 33546240 | bytes 33620992 | tf_op jit(solution)/shard_map/reduce_sum | solution.py:71
  225.7 29.8 %reduce-scatter.12.cloned.1.call-done = bf16[512,1024]{1,0:T(8,128)(2,1)} async-done(((bf16[1024,1024]{1,0:T(8,128)(2,1)}), bf16[512,1024]{1,0:T(8,128)(2,1)}) %reduce-scatter.12.cloned.1.call-update) | async-done | bytes 1048592 | tf_op jit(solution)/shard_map/reduce_scatter | solution.py:116
  260.4 11.1 %reduce-scatter.16.cloned.1.call-start = ((), (), s32[]{:S(2)}) async-start(), calls=%async_computation.17 | async-start | bytes 3145728 | tf_op jit(solution)/shard_map/reduce_scatter | solution.py:125
  273.1 24.7 %collective-permute-done = bf16[512,1024]{1,0:T(8,128)(2,1)} collective-permute-done((bf16[512,1024]{1,0:T(8,128)(2,1)}, bf16[512,1024]{1,0:T(8,128)(2,1)}, u32[]{:S(2)}, u32[]{:S(2)}) %collective-permute-start) | collective-permute-done | bytes 1048608 | tf_op jit(solution)/shard_map/ppermute | solution.py:19
  307.9 33.6 %all-gather.14.cloned.1.call-done = bf16[1024,1024]{1,0:T(8,128)(2,1)} async-done(((bf16[512,1024]{1,0:T(8,128)(2,1)}), bf16[1024,1024]{1,0:T(8,128)(2,1)}) %all-gather.14.cloned.1.call-update) | async-done | bytes 2097168 | tf_op jit(solution)/shard_map/all_gather | solution.py:100
  341.6 10.2 multiply_convert_fusion.1
  351.7 42.4 %all-gather.18.cloned.1.call-done = bf16[2048,1024]{0,1:T(8,128)(2,1)} async-done(((bf16[2048,64]{0,1:T(8,128)(2,1)}), bf16[2048,1024]{0,1:T(8,128)(2,1)}) %all-gather.18.cloned.1.call-update) | async-done | bytes 4194320 | tf_op jit(solution)/shard_map/all_gather | solution.py:141
  394.1 10.8 %fusion.56 = (f32[2048]{0:T(1024)S(1)}, bf16[1024,2048]{1,0:T(8,128)(2,1)S(1)}) fusion(f32[1024,2048]{1,0:T(8,128)} %get-tuple-element.37, f32[2048]{0:T(1024)S(1)} %dynamic_slice.14, bf16[1024,1024]{1,0:T(8,128)(2,1)} %fusion.39, bf16[2048,1024]{0,1:T(8,128)(2,1)} %all-gather.18.cloned.1.call-done), kind=kOutput, calls=%fused_computation.129 | convolution fusion | flops 4320131072 | bytes 18890752 | tf_op jit(solution)/shard_map/dot_general | solution.py:49
  422.2 21.2 %reduce-scatter.16.cloned.1.call-done = bf16[512,1024]{1,0:T(8,128)(2,1)} async-done(((bf16[1024,1024]{1,0:T(8,128)(2,1)}), bf16[512,1024]{1,0:T(8,128)(2,1)}) %reduce-scatter.16.cloned.1.call-update) | async-done | bytes 1048592 | tf_op jit(solution)/shard_map/reduce_scatter | solution.py:125
  445.8 31.7 %reduce-scatter.14.cloned.1.call-done = bf16[512,1024]{1,0:T(8,128)(2,1)} async-done(((bf16[1024,1024]{1,0:T(8,128)(2,1)}), bf16[512,1024]{1,0:T(8,128)(2,1)}) %reduce-scatter.14.cloned.1.call-update) | async-done | bytes 1048592 | tf_op jit(solution)/shard_map/reduce_scatter | solution.py:116
  484.4 24.4 %collective-permute-done.1 = bf16[512,1024]{1,0:T(8,128)(2,1)S(1)} collective-permute-done((bf16[512,1024]{1,0:T(8,128)(2,1)S(1)}, bf16[512,1024]{1,0:T(8,128)(2,1)S(1)}, u32[]{:S(2)}, u32[]{:S(2)}) %collective-permute-start.1) | collective-permute-done | bytes 1048608 | tf_op jit(solution)/shard_map/ppermute | solution.py:19
  515.9 12.3 %bitcast_convert_fusion = (bf16[1024,8,64]{0,2,1:T(8,128)(2,1)}, f32[8,64,1024]{2,1,0:T(8,128)S(1)}) fusion(bf16[1024,8,64]{0,2,1:T(8,128)(2,1)} %bitcast.194, bf16[8,1024,1024]{1,2,0:T(8,128)(2,1)} %fusion), kind=kOutput, calls=%fused_computation.72 | convolution fusion | flops 1074266112 | bytes 20971520 | tf_op jit(solution)/shard_map/hqk,qhe->khe/dot_general | solution.py:80
  528.1 21.0 %multiply_convert_fusion = bf16[8,1024,1024]{1,2,0:T(8,128)(2,1)} fusion(f32[8,1024,1024]{1,2,0:T(8,128)} %get-tuple-element.35, f32[8,1024]{1,0:T(8,128)S(1)} %get-tuple-element.38, f32[8,1024]{1,0:T(8,128)S(1)} %log_add_fusion, pred[1024]{0:T(1024)(128)(4,1)S(1)} %iota_compare_fusion, bf16[1024,8,64]{0,2,1:T(8,128)(2,1)} %bitcast.195, ...), kind=kOutput, calls=%fused_computation | convolution fusion | flops 1124073472 | bytes 52495360 | tf_op jit(solution)/shard_map/qhe,khe->hqk/dot_general | solution.py:83
  549.2 12.3 %multiply_convert_fusion.2 = bf16[8,64,1024]{2,1,0:T(8,128)(2,1)} fusion(bf16[1024,8,64]{0,2,1:T(8,128)(2,1)} %bitcast.182, bf16[8,1024,1024]{1,2,0:T(8,128)(2,1)} %multiply_convert_fusion), kind=kOutput, calls=%fused_computation.78 | convolution fusion | flops 1074790400 | bytes 18874368 | tf_op jit(solution)/shard_map/hqk,qhe->khe/dot_general | solution.py:93
  561.5 10.6 %bitcast_convert_fusion.1 = (bf16[1024,8,64]{0,2,1:T(8,128)(2,1)S(1)}, f32[8,64,1024]{2,1,0:T(8,128)}) fusion(bf16[1024,8,64]{0,2,1:T(8,128)(2,1)} %bitcast.180, bf16[8,1024,1024]{1,2,0:T(8,128)(2,1)} %multiply_convert_fusion), kind=kOutput, calls=%fused_computation.74 | convolution fusion | flops 1074790400 | bytes 20971520 | tf_op jit(solution)/shard_map/hqk,khe->qhe/dot_general | solution.py:90
  616.9 69.2 %reduce-scatter.24.cloned.1.call-done = bf16[64,2048]{1,0:T(8,128)(2,1)} async-done(((bf16[1024,2048]{1,0:T(8,128)(2,1)}), bf16[64,2048]{1,0:T(8,128)(2,1)}) %reduce-scatter.24.cloned.1.call-update) | async-done | bytes 262160 | tf_op jit(solution)/shard_map/reduce_scatter | solution.py:279
  688.0 73.8 %reduce-scatter.26.cloned.1.call-done = bf16[2048,64]{0,1:T(8,128)(2,1)} async-done(((bf16[2048,1024]{0,1:T(8,128)(2,1)}), bf16[2048,64]{0,1:T(8,128)(2,1)}) %reduce-scatter.26.cloned.1.call-update) | async-done | bytes 262160 | tf_op jit(solution)/shard_map/reduce_scatter | solution.py:282
  763.5 58.4 %reduce-scatter.22.cloned.1.call-done = bf16[512,64]{0,1:T(8,128)(2,1)} async-done(((bf16[512,1024]{0,1:T(8,128)(2,1)}), bf16[512,64]{0,1:T(8,128)(2,1)}) %reduce-scatter.22.cloned.1.call-update) | async-done | bytes 65552 | tf_op jit(solution)/shard_map/reduce_scatter | solution.py:276
  826.7 132.0 %reduce-scatter.28.cloned.1.call-done = f32[32,14]{1,0:T(8,128)} async-done(((f32[1024,14]{1,0:T(8,128)}), f32[32,14]{1,0:T(8,128)}) %reduce-scatter.28.cloned.1.call-update) | async-done | bytes 1808
  960.1 64.7 %reduce-scatter.20.cloned.1.call-done = bf16[3,64,512]{2,1,0:T(8,128)(2,1)} async-done(((bf16[3,1024,512]{2,1,0:T(8,128)(2,1)}), bf16[3,64,512]{2,1,0:T(8,128)(2,1)}) %reduce-scatter.20.cloned.1.call-update) | async-done | bytes 196624 | tf_op jit(solution)/shard_map/reduce_scatter | solution.py:273
  (166 shorter events, 148.5 us)
Async XLA Ops:
  7.2 73.2 %copy-start.1 = (bf16[1,512,1024]{2,1,0:T(8,128)(2,1)S(1)}, bf16[1,512,1024]{2,1,0:T(8,128)(2,1)}, u32[]{:S(2)}) copy-start(bf16[1,512,1024]{2,1,0:T(8,128)(2,1)} %param.10) | copy-start | bytes 3145732
  7.2 104.2 %all-gather.8.cloned.1.call-start = ((), (), s32[]{:S(2)}) async-start(), calls=%async_computation.9 | async-start | bytes 3145728 | tf_op jit(solution)/shard_map/all_gather | solution.py:100
  80.8 81.6 %copy-start.25 = (f32[512]{0:T(512)}, f32[512]{0:T(512)S(1)}, u32[]{:S(2)}) copy-start(f32[512]{0:T(512)S(1)} %add_rsqrt_fusion.1) | copy-start | bytes 6148
  82.3 76.8 %all-gather.10.cloned.1.call-start = ((), (), s32[]{:S(2)}) async-start(), calls=%async_computation.10 | async-start | bytes 3342336 | tf_op jit(solution)/shard_map/all_gather | solution.py:138
  83.0 137.8 %all-gather.12.cloned.1.call-start = ((), (), s32[]{:S(2)}) async-start(), calls=%async_computation.11 | async-start | bytes 1114112 | tf_op jit(solution)/shard_map/all_gather | solution.py:139
  83.8 171.7 %reduce-scatter.12.cloned.1.call-start = ((), (), s32[]{:S(2)}) async-start(), calls=%async_computation.12 | async-start | bytes 3145728 | tf_op jit(solution)/shard_map/reduce_scatter | solution.py:116
  163.9 14.2 %copy-start.6 = (bf16[1024,512]{0,1:T(8,128)(2,1)}, bf16[1024,512]{0,1:T(8,128)(2,1)S(1)}, u32[]{:S(2)}) copy-start(bf16[1024,512]{0,1:T(8,128)(2,1)S(1)} %add_convert_fusion.3) | copy-start | bytes 3145732
  178.1 20.5 %copy-start = (f32[8,1024,1024]{1,2,0:T(8,128)S(1)}, f32[8,1024,1024]{1,2,0:T(8,128)}, u32[]{:S(2)}) copy-start(f32[8,1024,1024]{1,2,0:T(8,128)} %get-tuple-element.35) | copy-start | bytes 100663296
  225.1 82.8 %all-gather.16.cloned.1.call-start = ((), (), s32[]{:S(2)}) async-start(), calls=%async_computation.14 | async-start | bytes 4456448 | tf_op jit(solution)/shard_map/all_gather | solution.py:140
  225.7 115.9 %all-gather.14.cloned.1.call-start = ((), (), s32[]{:S(2)}) async-start(), calls=%async_computation.13 | async-start | bytes 3145728 | tf_op jit(solution)/shard_map/all_gather | solution.py:100
  259.6 134.5 %all-gather.18.cloned.1.call-start = ((), (), s32[]{:S(2)}) async-start(), calls=%async_computation.15 | async-start | bytes 4456448 | tf_op jit(solution)/shard_map/all_gather | solution.py:141
  260.4 182.9 %reduce-scatter.16.cloned.1.call-start = ((), (), s32[]{:S(2)}) async-start(), calls=%async_computation.17 | async-start | bytes 3145728 | tf_op jit(solution)/shard_map/reduce_scatter | solution.py:125
  272.7 25.1 %collective-permute-start = (bf16[512,1024]{1,0:T(8,128)(2,1)}, bf16[512,1024]{1,0:T(8,128)(2,1)}, u32[]{:S(2)}, u32[]{:S(2)}) collective-permute-start(bf16[512,1024]{1,0:T(8,128)(2,1)} %fusion.20), channel_id=1, source_target_pairs={{0,1},{1,0},{2,3},{3,2},{4,5},{5,4},{6,7},{7,6},{8,9},{9,8},{10,11... | collective-permute-start | bytes 3145736 | tf_op jit(solution)/shard_map/ppermute | solution.py:19
  412.7 64.8 %reduce-scatter.14.cloned.1.call-start = ((), (), s32[]{:S(2)}) async-start(), calls=%async_computation.16 | async-start | bytes 3145728 | tf_op jit(solution)/shard_map/reduce_scatter | solution.py:116
  422.1 188.1 %reduce-scatter.18.cloned.1.call-start = ((), (), s32[]{:S(2)}) async-start(), calls=%async_computation.18 | async-start | bytes 3145728 | tf_op jit(solution)/shard_map/reduce_scatter | solution.py:125
  483.9 29.6 %copy-start.12 = (bf16[8,64,1024]{2,1,0:T(8,128)(2,1)S(1)}, bf16[8,64,1024]{2,1,0:T(8,128)(2,1)}, u32[]{:S(2)}) copy-start(bf16[8,64,1024]{2,1,0:T(8,128)(2,1)} %copy-done.11) | copy-start | bytes 3145732
  483.9 29.6 %copy-start.30 = (bf16[512,1024]{0,1:T(8,128)(2,1)S(1)}, bf16[512,1024]{0,1:T(8,128)(2,1)}, u32[]{:S(2)}) copy-start(bf16[512,1024]{0,1:T(8,128)(2,1)} %all-gather.12.cloned.1.call-done) | copy-start | bytes 3145732
  484.0 24.8 %collective-permute-start.1 = (bf16[512,1024]{1,0:T(8,128)(2,1)S(1)}, bf16[512,1024]{1,0:T(8,128)(2,1)S(1)}, u32[]{:S(2)}, u32[]{:S(2)}) collective-permute-start(bf16[512,1024]{1,0:T(8,128)(2,1)S(1)} %multiply_convert_fusion.3), channel_id=1, source_target_pairs={{0,1},{1,0},{2,3},{3,2},{4,5},{5,4},{6,7},{7,6},{8,9},{9,8},{10,11... | collective-permute-start | bytes 3145736 | tf_op jit(solution)/shard_map/ppermute | solution.py:19
  577.4 108.8 %reduce-scatter.24.cloned.1.call-start = ((), (), s32[]{:S(2)}) async-start(), calls=%async_computation.21 | async-start | bytes 4456448 | tf_op jit(solution)/shard_map/reduce_scatter | solution.py:279
  587.0 174.7 %reduce-scatter.26.cloned.1.call-start = ((), (), s32[]{:S(2)}) async-start(), calls=%async_computation.22 | async-start | bytes 4456448 | tf_op jit(solution)/shard_map/reduce_scatter | solution.py:282
  596.5 225.5 %reduce-scatter.22.cloned.1.call-start = ((), (), s32[]{:S(2)}) async-start(), calls=%async_computation.20 | async-start | bytes 1114112 | tf_op jit(solution)/shard_map/reduce_scatter | solution.py:276
  603.0 355.7 %reduce-scatter.28.cloned.1.call-start = ((), (), s32[]{:S(2)}) async-start(), calls=%async_computation.23 | async-start | bytes 540672
  613.6 411.2 %reduce-scatter.20.cloned.1.call-start = ((), (), s32[]{:S(2)}) async-start(), calls=%async_computation.19 | async-start | bytes 3342336 | tf_op jit(solution)/shard_map/reduce_scatter | solution.py:273
  616.9 206.5 %copy-start.4 = (f32[512,1024]{1,0:T(8,128)S(1)}, f32[512,1024]{1,0:T(8,128)}, u32[]{:S(2)}) copy-start(f32[512,1024]{1,0:T(8,128)} %copy-done.3) | copy-start | bytes 6291460
  (25 other events, 97.4 us)
Sparse Core Ops, SparseCore 0:
  82.4 28.9 all-gather.7
  113.6 45.4 all-gather.9
  161.3 36.1 all-gather.11
  225.2 30.2 reduce-scatter.11
  257.5 50.3 all-gather.15
  309.9 31.6 all-gather.13
  343.7 50.3 all-gather.17
  412.8 30.4 reduce-scatter.15
  445.6 31.8 reduce-scatter.13
  577.5 31.8 reduce-scatter.17
  613.3 72.8 reduce-scatter.23
  689.9 71.8 reduce-scatter.25
  765.4 56.5 reduce-scatter.21
  824.0 134.6 reduce-scatter.27
  962.4 62.3 reduce-scatter.19
